TPU v7x, 32 devices: a whole 2x2x4 slice. The times are simulated.
32 devices in a mesh: gx: 8 (over y, x, core), gy: 4 (over z).
Axes of the slice: x: 2, y: 2, z: 4, core: 2. Of those that a mesh axis runs over, the one named last changes fastest.
Arguments:
- block_input: bfloat16 [25088, 512], P(('gx', 'gy')), may hold values from -6 to 6
- cotangent: bfloat16 [25088, 512], P(('gx', 'gy')), may hold values from -6 to 6
- live_images: int32 [8], P('gx'), may hold values from 1 to 16, 96 in all
- ln1_gain: bfloat16 [512], replicated, may hold values from 0.25 to 1.75
- ln1_bias: bfloat16 [512], replicated, may hold values from -3 to 3
- qkv_weight: bfloat16 [512, 3, 512], P('gx', None, 'gy'), may hold values from -0.25 to 0.25
- qv_bias: bfloat16 [2, 512], P(None, 'gy'), may hold values from -3 to 3
- rel_table: bfloat16 [169, 16], P(None, 'gy'), may hold values from -4 to 254
- proj_weight: bfloat16 [512, 512], P('gy', 'gx'), may hold values from -0.75 to 0.75
- proj_bias: bfloat16 [512], replicated, may hold values from -3 to 3
- ln2_gain: bfloat16 [512], replicated, may hold values from 0.25 to 1.75
- ln2_bias: bfloat16 [512], replicated, may hold values from -3 to 3
- fc1_weight: bfloat16 [512, 2048], P('gx', 'gy'), may hold values from -0.25 to 0.25
- fc1_bias: bfloat16 [2048], P('gy'), may hold values from -3 to 3
- fc2_weight: bfloat16 [2048, 512], P('gy', 'gx'), may hold values from -0.1875 to 0.1875
- fc2_bias: bfloat16 [512], replicated, may hold values from -3 to 3
Outputs:
- output: bfloat16 [25088, 512], P(('gx', 'gy'))
- d_input: bfloat16 [25088, 512], P(('gx', 'gy'))
- d_ln1_gain: float32 [512], replicated
- d_ln1_bias: float32 [512], replicated
- d_qkv_weight: float32 [512, 3, 512], P('gx', None, 'gy')
- d_qv_bias: float32 [2, 512], P(None, 'gy')
- d_rel_table: float32 [169, 16], P(None, 'gy')
- d_proj_weight: float32 [512, 512], P('gy', 'gx')
- d_proj_bias: float32 [512], replicated
- d_ln2_gain: float32 [512], replicated
- d_ln2_bias: float32 [512], replicated
- d_fc1_weight: float32 [512, 2048], P('gx', 'gy')
- d_fc1_bias: float32 [2048], P('gy')
- d_fc2_weight: float32 [2048, 512], P('gy', 'gx')
- d_fc2_bias: float32 [512], replicated
Inputs may be any that keep to these rules, and one draw needn't show every extreme that they name: Image slot s of index i of gx (slots 0 to 15 in order) holds an image exactly when s < live_images[i]; the counts add up to 96.
All inputs are finite; a program needn't handle non-finite values. No bound on the sum of `live_images` on one device may be relied on, other than what follows from the above.
Results may differ from a plain program's by a relative error of at most 0.014.
Values may be sent and summed in bfloat16 or wider, within the bound.
A program may use at most 192 MiB of HBM per device.

v0:
```python
import jax
import jax.numpy as jnp
from jax import lax
from jax.sharding import PartitionSpec as P

HD = 32
GRID = 14
WIN = 7
SHIFT = 3
RELS = 169


eps_norm = 1e-05
mask_value = -100.0
inv_root_two = 0.7071067811865476
inv_root_two_pi = 0.3989422804014327


def matmul(left, right):
    return jnp.dot(left, right, preferred_element_type=jnp.float32)


def matmul_tn(left, right):
    return lax.dot_general(
        left, right, (((0,), (0,)), ((), ())), preferred_element_type=jnp.float32
    )


def matmul_nt(left, right):
    return lax.dot_general(
        left, right, (((1,), (1,)), ((), ())), preferred_element_type=jnp.float32
    )


def window_tables():
    win_area = WIN * WIN
    places = jnp.arange(win_area, dtype=jnp.int32)
    in_row = places // WIN
    in_col = places % WIN
    rel_index = (in_row[:, None] - in_row[None, :] + WIN - 1) * (2 * WIN - 1) + (
        in_col[:, None] - in_col[None, :] + WIN - 1
    )
    onehot = (rel_index[:, :, None] == jnp.arange(RELS, dtype=jnp.int32)[None, None, :]).astype(
        jnp.float32
    )
    win_count = GRID // WIN
    cells = jnp.arange(GRID, dtype=jnp.int32)
    region = jnp.where(cells < GRID - WIN, 0, jnp.where(cells < GRID - SHIFT, 1, 2))
    cell_id = region[:, None] * 3 + region[None, :]
    win_id = (
        cell_id.reshape(win_count, WIN, win_count, WIN)
        .transpose(0, 2, 1, 3)
        .reshape(win_count, win_count, win_area)
    )
    shift_mask = jnp.where(win_id[:, :, :, None] == win_id[:, :, None, :], 0.0, mask_value).astype(
        jnp.float32
    )
    return (onehot, shift_mask)


def to_windows(values, head_count):
    image_count = values.shape[0] // (GRID * GRID)
    win_count = GRID // WIN
    cells = values.reshape(image_count, GRID, GRID, head_count, HD)
    cells = jnp.roll(cells, (-SHIFT, -SHIFT), axis=(1, 2))
    cells = cells.reshape(image_count, win_count, WIN, win_count, WIN, head_count, HD)
    return cells.transpose(0, 1, 3, 5, 2, 4, 6).reshape(
        image_count, win_count, win_count, head_count, WIN * WIN, HD
    )


def from_windows(windows):
    image_count, win_count, win_other, head_count = windows.shape[:4]
    cells = windows.reshape(image_count, win_count, win_other, head_count, WIN, WIN, HD).transpose(
        0, 1, 4, 2, 5, 3, 6
    )
    cells = cells.reshape(image_count, GRID, GRID, head_count, HD)
    cells = jnp.roll(cells, (SHIFT, SHIFT), axis=(1, 2))
    return cells.reshape(image_count * GRID * GRID, head_count * HD)


def window_scores(query_win, keys_win, table, onehot, shift_mask):
    raw = jnp.einsum(
        "nabhid,nabhjd->nabhij", query_win, keys_win, preferred_element_type=jnp.float32
    ) * HD ** (-0.5)
    bias = jnp.einsum("rh,ijr->hij", table, onehot, precision=lax.Precision.HIGHEST)
    return raw + bias[None, None, None] + shift_mask[None, :, :, None]


def attend_forward(query, keys, values, table, onehot, shift_mask, head_count):
    query_win = to_windows(query, head_count)
    keys_win = to_windows(keys, head_count)
    values_win = to_windows(values, head_count)
    scores = window_scores(query_win, keys_win, table, onehot, shift_mask)
    row_top = jnp.max(scores, -1, keepdims=True)
    log_total = row_top + jnp.log(jnp.sum(jnp.exp(scores - row_top), -1, keepdims=True))
    probs = jnp.exp(scores - log_total).astype(jnp.bfloat16)
    context = jnp.einsum(
        "nabhij,nabhjd->nabhid", probs, values_win, preferred_element_type=jnp.float32
    )
    return (from_windows(context).astype(jnp.bfloat16), log_total)


def attend_backward(
    query, keys, values, log_total, d_context, table, onehot, shift_mask, head_count
):
    query_win = to_windows(query, head_count)
    keys_win = to_windows(keys, head_count)
    values_win = to_windows(values, head_count)
    scores = window_scores(query_win, keys_win, table, onehot, shift_mask)
    probs = jnp.exp(scores - log_total)
    d_win = to_windows(d_context, head_count)
    d_probs = jnp.einsum(
        "nabhid,nabhjd->nabhij", d_win, values_win, preferred_element_type=jnp.float32
    )
    d_values = jnp.einsum(
        "nabhij,nabhid->nabhjd",
        probs.astype(jnp.bfloat16),
        d_win,
        preferred_element_type=jnp.float32,
    )
    row_dot = jnp.sum(probs * d_probs, -1, keepdims=True)
    d_scores = probs * (d_probs - row_dot)
    d_table = jnp.einsum(
        "hij,ijr->rh", jnp.sum(d_scores, (0, 1, 2)), onehot, precision=lax.Precision.HIGHEST
    )
    d_scores_low = d_scores.astype(jnp.bfloat16)
    score_scale = HD ** (-0.5)
    d_query = (
        jnp.einsum(
            "nabhij,nabhjd->nabhid", d_scores_low, keys_win, preferred_element_type=jnp.float32
        )
        * score_scale
    )
    d_keys = (
        jnp.einsum(
            "nabhij,nabhid->nabhjd", d_scores_low, query_win, preferred_element_type=jnp.float32
        )
        * score_scale
    )
    return (from_windows(d_query), from_windows(d_keys), from_windows(d_values), d_table)


def gelu_parts(pre_act):
    cdf_part = 0.5 * (1.0 + jax.scipy.special.erf(pre_act * inv_root_two))
    return (
        pre_act * cdf_part,
        cdf_part + pre_act * jnp.exp(-0.5 * pre_act * pre_act) * inv_root_two_pi,
    )


def layer_norm(rows, gain, shift):
    row_mean = jnp.mean(rows, -1, keepdims=True)
    row_var = jnp.mean(rows * rows, -1, keepdims=True) - row_mean * row_mean
    inv_std = lax.rsqrt(row_var + eps_norm)
    normed = (rows - row_mean) * inv_std
    return (normed, inv_std, normed * gain + shift)


def norm_back(d_out, normed, inv_std, gain):
    d_normed = d_out * gain
    return inv_std * (
        d_normed
        - jnp.mean(d_normed, -1, keepdims=True)
        - normed * jnp.mean(d_normed * normed, -1, keepdims=True)
    )


def full_rows(part_rows):
    return lax.all_gather(part_rows, "gy", axis=0, tiled=True)


def share_rows(term):
    return lax.psum_scatter(term, "gy", scatter_dimension=0, tiled=True)


def local_live(tok_local, live_images):
    position = lax.axis_index("gy")
    per_device = tok_local // (GRID * GRID)
    slot_index = position * per_device + jnp.arange(tok_local, dtype=jnp.int32) // (GRID * GRID)
    return slot_index < live_images[0]


def blocked_layer(block_input, cotangent, live_images, params, onehot, shift_mask):
    (
        ln1_gain,
        ln1_bias,
        qkv_weight,
        qv_bias,
        rel_table,
        proj_weight,
        proj_bias,
        ln2_gain,
        ln2_bias,
        fc1_weight,
        fc1_bias,
        fc2_weight,
        fc2_bias,
    ) = params
    tok_local, width = block_input.shape
    feat_local = qkv_weight.shape[2]
    head_local = rel_table.shape[1]
    qkv_rows, fc1_rows, proj_cols, fc2_cols = (
        lax.all_gather(qkv_weight, "gx", axis=0, tiled=True),
        lax.all_gather(fc1_weight, "gx", axis=0, tiled=True),
        lax.all_gather(proj_weight, "gx", axis=1, tiled=True),
        lax.all_gather(fc2_weight, "gx", axis=1, tiled=True),
    )
    qkv_flat = qkv_rows.reshape(width, 3 * feat_local)
    gain_one = ln1_gain.astype(jnp.float32)
    gain_two = ln2_gain.astype(jnp.float32)
    resid = block_input.astype(jnp.float32)
    normed_one, scale_one, pre_one = layer_norm(resid, gain_one, ln1_bias.astype(jnp.float32))
    hidden_one = full_rows(pre_one.astype(jnp.bfloat16))
    tok_count = hidden_one.shape[0]
    mixed = matmul(hidden_one, qkv_flat).reshape(tok_count, 3, feat_local)
    bias_pair = qv_bias.astype(jnp.float32)
    query = (mixed[:, 0] + bias_pair[0]).astype(jnp.bfloat16)
    keys = mixed[:, 1].astype(jnp.bfloat16)
    values = (mixed[:, 2] + bias_pair[1]).astype(jnp.bfloat16)
    table = rel_table.astype(jnp.float32)
    context, log_total = attend_forward(query, keys, values, table, onehot, shift_mask, head_local)
    resid_one = resid + share_rows(matmul(context, proj_cols)) + proj_bias.astype(jnp.float32)
    normed_two, scale_two, pre_two = layer_norm(resid_one, gain_two, ln2_bias.astype(jnp.float32))
    hidden_two = full_rows(pre_two.astype(jnp.bfloat16))
    pre_act = matmul(hidden_two, fc1_rows) + fc1_bias.astype(jnp.float32)
    act_full, slope = gelu_parts(pre_act)
    act_low = act_full.astype(jnp.bfloat16)
    output = (
        resid_one + share_rows(matmul(act_low, fc2_cols)) + fc2_bias.astype(jnp.float32)
    ).astype(jnp.bfloat16)
    live_rows = local_live(tok_local, live_images)
    grad_out = jnp.where(live_rows[:, None], cotangent, jnp.zeros_like(cotangent))
    grad_float = grad_out.astype(jnp.float32)
    grad_full = full_rows(grad_out)
    d_fc2_bias = jnp.sum(grad_float, 0)
    d_fc2_weight = matmul_tn(act_low, grad_full)
    d_pre = matmul_nt(grad_full, fc2_cols) * slope
    d_fc1_bias = jnp.sum(d_pre, 0)
    d_pre_low = d_pre.astype(jnp.bfloat16)
    d_fc1_weight = matmul_tn(hidden_two, d_pre_low)
    d_hidden_two = share_rows(matmul_nt(d_pre_low, fc1_rows))
    d_ln2_gain = jnp.sum(d_hidden_two * normed_two, 0)
    d_ln2_bias = jnp.sum(d_hidden_two, 0)
    d_resid_one = grad_float + norm_back(d_hidden_two, normed_two, scale_two, gain_two)
    d_proj_bias = jnp.sum(d_resid_one, 0)
    d_resid_full = full_rows(d_resid_one.astype(jnp.bfloat16))
    d_proj_weight = matmul_tn(context, d_resid_full)
    d_context = matmul_nt(d_resid_full, proj_cols).astype(jnp.bfloat16)
    d_query, d_keys, d_values, d_table = attend_backward(
        query, keys, values, log_total, d_context, table, onehot, shift_mask, head_local
    )
    d_qv_bias = jnp.stack([jnp.sum(d_query, 0), jnp.sum(d_values, 0)])
    d_mixed = (
        jnp.stack([d_query, d_keys, d_values], 1)
        .astype(jnp.bfloat16)
        .reshape(tok_count, 3 * feat_local)
    )
    d_qkv_weight = matmul_tn(hidden_one, d_mixed).reshape(width, 3, feat_local)
    d_hidden_one = share_rows(matmul_nt(d_mixed, qkv_flat))
    d_ln1_gain = jnp.sum(d_hidden_one * normed_one, 0)
    d_ln1_bias = jnp.sum(d_hidden_one, 0)
    d_input = (d_resid_one + norm_back(d_hidden_one, normed_one, scale_one, gain_one)).astype(
        jnp.bfloat16
    )
    d_qkv_weight, d_fc1_weight, d_proj_weight, d_fc2_weight = (
        lax.psum_scatter(
            d_qkv_weight.astype(jnp.bfloat16), "gx", scatter_dimension=0, tiled=True
        ).astype(jnp.float32),
        lax.psum_scatter(
            d_fc1_weight.astype(jnp.bfloat16), "gx", scatter_dimension=0, tiled=True
        ).astype(jnp.float32),
        lax.psum_scatter(
            d_proj_weight.astype(jnp.bfloat16), "gx", scatter_dimension=1, tiled=True
        ).astype(jnp.float32),
        lax.psum_scatter(
            d_fc2_weight.astype(jnp.bfloat16), "gx", scatter_dimension=1, tiled=True
        ).astype(jnp.float32),
    )
    head_sums = lax.psum((d_qv_bias, d_table, d_fc1_bias), "gx")
    norm_sums = lax.psum(
        (d_ln1_gain, d_ln1_bias, d_proj_bias, d_ln2_gain, d_ln2_bias, d_fc2_bias), ("gx", "gy")
    )
    return (
        output,
        d_input,
        norm_sums[0],
        norm_sums[1],
        d_qkv_weight,
        head_sums[0],
        head_sums[1],
        d_proj_weight,
        norm_sums[2],
        norm_sums[3],
        norm_sums[4],
        d_fc1_weight,
        head_sums[2],
        d_fc2_weight,
        norm_sums[5],
    )


def shards(
    block_input,
    cotangent,
    live_images,
    ln1_gain,
    ln1_bias,
    qkv_weight,
    qv_bias,
    rel_table,
    proj_weight,
    proj_bias,
    ln2_gain,
    ln2_bias,
    fc1_weight,
    fc1_bias,
    fc2_weight,
    fc2_bias,
):
    onehot, shift_mask = window_tables()
    params = (
        ln1_gain,
        ln1_bias,
        qkv_weight,
        qv_bias,
        rel_table,
        proj_weight,
        proj_bias,
        ln2_gain,
        ln2_bias,
        fc1_weight,
        fc1_bias,
        fc2_weight,
        fc2_bias,
    )
    results = blocked_layer(block_input, cotangent, live_images, params, onehot, shift_mask)
    return results


def solution(mesh):
    return jax.shard_map(
        shards,
        mesh=mesh,
        in_specs=(
            P(("gx", "gy"), None),
            P(("gx", "gy"), None),
            P("gx"),
            P(),
            P(),
            P("gx", None, "gy"),
            P(None, "gy"),
            P(None, "gy"),
            P("gy", "gx"),
            P(),
            P(),
            P(),
            P("gx", "gy"),
            P("gy"),
            P("gy", "gx"),
            P(),
        ),
        out_specs=(
            P(("gx", "gy"), None),
            P(("gx", "gy"), None),
            P(),
            P(),
            P("gx", None, "gy"),
            P(None, "gy"),
            P(None, "gy"),
            P("gy", "gx"),
            P(),
            P(),
            P(),
            P("gx", "gy"),
            P("gy"),
            P("gy", "gx"),
            P(),
        ),
        check_vma=False,
    )
```

profile of v0, /device:TPU:0, one launch (start us, length us, event | category | flops | bytes accessed | tf_op | source)
XLA Modules:
  0.0 1064.7 jit_solution(1826730475348665473)
XLA Ops:
  10.7 2.4 fusion.28
  14.7 11.1 %all_gather.25 = bf16[512,3,128]{2,0,1:T(8,128)(2,1)S(1)} all-gather(bf16[64,3,128]{2,0,1:T(8,128)(2,1)S(1)} %copy-done.35), channel_id=1, replica_groups=mesh['gx'=8,'gy'=4] {'gx'}, dimensions={0}, use_global_device_ids=true | all-gather | bytes 442368 | tf_op jit(solution)/shard_map/all_gather | solution.py:204
  26.0 9.4 all_gather.26
  36.1 44.5 %all-gather.5.cloned.1.call-done = bf16[3136,512]{1,0:T(8,128)(2,1)} async-done(((bf16[784,512]{1,0:T(8,128)(2,1)}), bf16[3136,512]{1,0:T(8,128)(2,1)}) %all-gather.5.cloned.1.call-update) | async-done | bytes 3211280 | tf_op jit(solution)/shard_map/all_gather | solution.py:170
  80.5 3.8 fusion.13
  87.2 4.2 convert_element_type.117
  96.6 4.4 squeeze.10
  101.0 4.9 fusion.6
  106.5 6.2 squeeze.11
  112.7 4.9 fusion.5
  123.5 5.1 copy.112
  132.0 5.3 copy.111
  140.8 5.7 copy.117
  146.5 3.9 fusion.73
  150.4 2.4 exponential_reduce_fusion
  153.6 2.5 fusion.55
  156.1 4.3 copy.118
  164.5 2.4 convert_element_type.120
  167.0 4.9 fusion.75
  172.6 111.0 %reduce-scatter.9.cloned.1.call-done = f32[784,512]{1,0:T(8,128)} async-done(((f32[3136,512]{1,0:T(8,128)}), f32[784,512]{1,0:T(8,128)}) %reduce-scatter.9.cloned.1.call-update) | async-done | bytes 1605648 | tf_op jit(solution)/shard_map/reduce_scatter | solution.py:174
  288.7 9.8 all_gather.28
  298.5 9.8 all_gather.29
  308.3 43.6 %all-gather.7.cloned.1.call-done = bf16[3136,512]{1,0:T(8,128)(2,1)} async-done(((bf16[784,512]{1,0:T(8,128)(2,1)}), bf16[3136,512]{1,0:T(8,128)(2,1)}) %all-gather.7.cloned.1.call-update) | async-done | bytes 3211280 | tf_op jit(solution)/shard_map/all_gather | solution.py:170
  351.9 6.7 multiply_convert_fusion
  358.6 57.9 %all-gather.9.cloned.1.call-done = bf16[3136,512]{1,0:T(8,128)(2,1)} async-done(((bf16[784,512]{1,0:T(8,128)(2,1)}), bf16[3136,512]{1,0:T(8,128)(2,1)}) %all-gather.9.cloned.1.call-update) | async-done | bytes 3211280 | tf_op jit(solution)/shard_map/all_gather | solution.py:170
  416.5 6.3 fusion.74
  424.5 4.7 fusion.39
  429.3 7.0 fusion.76
  437.0 103.9 %reduce-scatter.13.cloned.1.call-done = f32[784,512]{1,0:T(8,128)} async-done(((f32[3136,512]{1,0:T(8,128)}), f32[784,512]{1,0:T(8,128)}) %reduce-scatter.13.cloned.1.call-update) | async-done | bytes 1605648 | tf_op jit(solution)/shard_map/reduce_scatter | solution.py:174
  543.2 113.3 %reduce-scatter.11.cloned.1.call-done = f32[784,512]{1,0:T(8,128)} async-done(((f32[3136,512]{1,0:T(8,128)}), f32[784,512]{1,0:T(8,128)}) %reduce-scatter.11.cloned.1.call-update) | async-done | bytes 1605648 | tf_op jit(solution)/shard_map/reduce_scatter | solution.py:174
  656.6 3.1 fusion.70
  661.9 5.8 convolution_convert_fusion.1
  667.8 4.9 fusion.43
  672.8 54.2 %all-gather.11.cloned.1.call-done = bf16[3136,512]{1,0:T(8,128)(2,1)} async-done(((bf16[784,512]{1,0:T(8,128)(2,1)}), bf16[3136,512]{1,0:T(8,128)(2,1)}) %all-gather.11.cloned.1.call-update) | async-done | bytes 3211280 | tf_op jit(solution)/shard_map/all_gather | solution.py:170
  727.0 3.8 convolution_convert_fusion
  730.8 4.6 reshape.378
  741.2 4.2 copy.124
  745.4 7.1 fusion.53
  752.5 6.6 copy.138
  759.2 3.8 copy.139
  764.1 2.7 slice.197
  767.0 2.6 multiply_reduce_fusion
  769.6 2.9 fusion.65
  772.5 3.3 convolution_multiply_fusion.1
  775.9 3.1 convolution_multiply_fusion.2
  779.0 4.3 copy.133
  784.9 6.7 copy.128
  791.5 3.6 copy.129
  798.3 3.0 fusion.66
  804.0 2.7 stack_reshape.10
  806.7 2.5 pad_maximum_fusion.2
  810.4 2.4 stack_reshape.9
  812.8 2.5 pad_maximum_fusion.3
  815.3 2.9 copy.140
  818.2 4.9 stack_reshape.11
  823.1 3.2 convolution_convert_fusion.2
  826.4 5.4 fusion.46
  831.9 4.6 convolution_bitcast_fusion
  841.1 14.4 %all-reduce.1 = (f32[2,128]{1,0:T(2,128)}, f32[169,4]{0,1:T(4,128)}, f32[512]{0:T(512)}) all-reduce(f32[2,128]{1,0:T(2,128)S(1)} %pad_maximum_fusion.14, f32[169,4]{0,1:T(4,128)S(1)} %fusion.52, f32[512]{0:T(512)S(1)} %get-tuple-element.66), channel_id=1, replica_groups=mesh['gx'=8,'gy'=4] {'gx'}, use_global_device_ids=true, to_apply=%region_24.25 | all-reduce | flops 1444 | bytes 11552 | tf_op jit(solution)/shard_map/psum | solution.py:280
  855.5 3.3 reduce-scatter.19.cloned.1.call-done
  860.1 36.2 %reduce-scatter.17.cloned.1.call-done = bf16[64,3,128]{2,0,1:T(8,128)(2,1)} async-done(((bf16[512,3,128]{2,0,1:T(8,128)(2,1)}), bf16[64,3,128]{2,0,1:T(8,128)(2,1)}) %reduce-scatter.17.cloned.1.call-update) | async-done | bytes 49168 | tf_op jit(solution)/shard_map/reduce_scatter | solution.py:267
  897.8 113.6 %reduce-scatter.15.cloned.1.call-done = f32[784,512]{1,0:T(8,128)} async-done(((f32[3136,512]{1,0:T(8,128)}), f32[784,512]{1,0:T(8,128)}) %reduce-scatter.15.cloned.1.call-update) | async-done | bytes 1605648 | tf_op jit(solution)/shard_map/reduce_scatter | solution.py:174
  1013.8 40.9 %all-reduce = (f32[512]{0:T(512)}, f32[512]{0:T(512)}, f32[512]{0:T(512)}, f32[512]{0:T(512)}, f32[512]{0:T(512)}, /*index=5*/f32[512]{0:T(512)}) all-reduce(f32[512]{0:T(512)S(1)} %get-tuple-element.17, f32[512]{0:T(512)S(1)} %get-tuple-element.22, f32[512]{0:T(512)S(1)} %get-tuple-element.50, ...), channel_id=1, replica_groups=mesh['gx'=8,'gy'=4] {'gx','gy'}, use_global_device_ids=true, to_apply=%region_16.17 | all-reduce | flops 3072 | bytes 24576 | tf_op jit(solution)/shard_map/psum | solution.py:281
  1054.7 2.9 fusion.33
  (226 shorter events, 69.7 us)
Async XLA Ops:
  7.2 6.6 copy-start
  7.2 6.0 copy-start.46
  7.2 7.5 copy-start.35
  7.2 18.7 %copy-start.40 = (bf16[128,64]{0,1:T(8,128)(2,1)S(1)}, bf16[128,64]{0,1:T(8,128)(2,1)}, u32[]{:S(2)}) copy-start(bf16[128,64]{0,1:T(8,128)(2,1)} %param.24) | copy-start | bytes 49156
  7.2 73.3 %all-gather.5.cloned.1.call-start = ((), (), s32[]{:S(2)}) async-start(), calls=%async_computation.8 | async-start | bytes 4014080 | tf_op jit(solution)/shard_map/all_gather | solution.py:170
  8.0 2.2 copy-start.36
  10.1 0.6 copy-start.31
  10.1 0.6 copy-start.33
  13.1 270.4 %reduce-scatter.9.cloned.1.call-start = ((), (), s32[]{:S(2)}) async-start(), calls=%async_computation.9 | async-start | bytes 8028160 | tf_op jit(solution)/shard_map/reduce_scatter | solution.py:174
  13.8 0.8 copy-start.38
  25.8 58.5 %copy-start.22 = (bf16[512,3,128]{2,0,1:T(8,128)(2,1)}, bf16[512,3,128]{2,0,1:T(8,128)(2,1)S(1)}, u32[]{:S(2)}) copy-start(bf16[512,3,128]{2,0,1:T(8,128)(2,1)S(1)} %all_gather.25) | copy-start | bytes 1179652
  93.5 3.0 copy-start.17
  117.6 3.0 copy-start.15
  117.6 3.0 copy-start.21
  132.0 5.3 copy-start.3
  132.0 5.3 copy-start.18
  140.8 5.7 copy-start.7
  140.8 5.7 copy-start.28
  150.4 3.2 copy-start.2
  150.4 3.2 copy-start.9
  171.9 0.7 copy-start.41
  171.9 0.7 copy-start.42
  171.9 0.7 copy-start.43
  171.9 111.7 %copy-start.5 = (bf16[784,512]{1,0:T(8,128)(2,1)S(1)}, bf16[784,512]{1,0:T(8,128)(2,1)}, u32[]{:S(2)}) copy-start(bf16[784,512]{1,0:T(8,128)(2,1)} %param.16) | copy-start | bytes 2408452
  171.9 180.0 %all-gather.7.cloned.1.call-start = ((), (), s32[]{:S(2)}) async-start(), calls=%async_computation.10 | async-start | bytes 4014080 | tf_op jit(solution)/shard_map/all_gather | solution.py:170
  172.6 114.9 %copy-start.24 = (bf16[784,512]{1,0:T(8,128)(2,1)S(1)}, bf16[784,512]{1,0:T(8,128)(2,1)}, u32[]{:S(2)}) copy-start(bf16[784,512]{1,0:T(8,128)(2,1)} %param.17) | copy-start | bytes 2408452
  285.4 3.2 copy-start.44
  285.4 3.3 copy-start.29
  285.5 13.1 %copy-start.30 = (bf16[512,64]{0,1:T(8,128)(2,1)S(1)}, bf16[512,64]{0,1:T(8,128)(2,1)}, u32[]{:S(2)}) copy-start(bf16[512,64]{0,1:T(8,128)(2,1)} %param.30) | copy-start | bytes 196612
  286.7 129.8 %all-gather.9.cloned.1.call-start = ((), (), s32[]{:S(2)}) async-start(), calls=%async_computation.12 | async-start | bytes 4014080 | tf_op jit(solution)/shard_map/all_gather | solution.py:170
  288.6 252.3 %reduce-scatter.13.cloned.1.call-start = ((), (), s32[]{:S(2)}) async-start(), calls=%async_computation.13 | async-start | bytes 8028160 | tf_op jit(solution)/shard_map/reduce_scatter | solution.py:174
  422.9 1.6 copy-start.19
  429.2 227.3 %reduce-scatter.11.cloned.1.call-start = ((), (), s32[]{:S(2)}) async-start(), calls=%async_computation.11 | async-start | bytes 8028160 | tf_op jit(solution)/shard_map/reduce_scatter | solution.py:174
  436.3 0.7 copy-start.45
  436.3 220.2 %copy-start.16 = (bf16[784,512]{1,0:T(8,128)(2,1)S(1)}, bf16[784,512]{1,0:T(8,128)(2,1)}, u32[]{:S(2)}) copy-start(bf16[784,512]{1,0:T(8,128)(2,1)} %get-tuple-element.49) | copy-start | bytes 2408452
  436.3 290.7 %all-gather.11.cloned.1.call-start = ((), (), s32[]{:S(2)}) async-start(), calls=%async_computation.14 | async-start | bytes 4014080 | tf_op jit(solution)/shard_map/all_gather | solution.py:170
  659.6 1.2 copy-start.12
  661.8 5.9 copy-start.20
  661.9 174.8 %reduce-scatter.23.cloned.1.call-start = ((), (), s32[]{:S(2)}) async-start(), calls=%async_computation.19 | async-start | bytes 589824 | tf_op jit(solution)/shard_map/reduce_scatter | solution.py:276
  667.7 170.5 %reduce-scatter.21.cloned.1.call-start = ((), (), s32[]{:S(2)}) async-start(), calls=%async_computation.18 | async-start | bytes 589824 | tf_op jit(solution)/shard_map/reduce_scatter | solution.py:270
  672.7 186.0 %reduce-scatter.19.cloned.1.call-start = ((), (), s32[]{:S(2)}) async-start(), calls=%async_computation.17 | async-start | bytes 147456 | tf_op jit(solution)/shard_map/reduce_scatter | solution.py:273
  759.2 7.6 slice-start
  762.9 3.9 slice-start.1
  764.1 2.9 copy-start.10
  769.6 2.9 copy-start.11
  772.5 3.4 copy-start.8
  795.2 2.2 slice-start.2
  795.3 2.3 slice-start.3
  796.1 2.1 copy-start.14
  818.2 4.9 copy-start.4
  826.3 5.6 copy-start.23
  826.3 5.6 copy-start.25
  826.3 5.6 copy-start.26
  826.4 5.6 copy-start.27
  826.4 70.0 %reduce-scatter.17.cloned.1.call-start = ((), (), s32[]{:S(2)}) async-start(), calls=%async_computation.16 | async-start | bytes 442368 | tf_op jit(solution)/shard_map/reduce_scatter | solution.py:267
  831.9 179.6 %reduce-scatter.15.cloned.1.call-start = ((), (), s32[]{:S(2)}) async-start(), calls=%async_computation.15 | async-start | bytes 8028160 | tf_op jit(solution)/shard_map/reduce_scatter | solution.py:174
  836.5 3.6 copy-start.39
  836.5 174.9 %copy-start.6 = (bf16[784,512]{1,0:T(8,128)(2,1)S(1)}, bf16[784,512]{1,0:T(8,128)(2,1)}, u32[]{:S(2)}) copy-start(bf16[784,512]{1,0:T(8,128)(2,1)} %param.16) | copy-start | bytes 2408452
  836.5 174.9 %copy-start.32 = (f32[784]{0:T(1024)S(1)}, f32[784]{0:T(1024)}, u32[]{:S(2)}) copy-start(f32[784]{0:T(1024)} %copy-done.31) | copy-start | bytes 9412
  836.5 174.9 %copy-start.34 = (f32[784]{0:T(1024)S(1)}, f32[784]{0:T(1024)}, u32[]{:S(2)}) copy-start(f32[784]{0:T(1024)} %copy-done.33) | copy-start | bytes 9412
  836.5 174.9 %copy-start.37 = (f32[512]{0:T(512)S(1)}, f32[512]{0:T(512)}, u32[]{:S(2)}) copy-start(f32[512]{0:T(512)} %copy-done.36) | copy-start | bytes 6148
  836.6 218.1 %copy-start.13 = (f32[784,512]{1,0:T(8,128)S(1)}, f32[784,512]{1,0:T(8,128)}, u32[]{:S(2)}) copy-start(f32[784,512]{1,0:T(8,128)} %copy-done.12) | copy-start | bytes 4816900
  896.3 161.2 %copy-start.1 = (bf16[169,4]{0,1:T(4,128)(2,1)S(1)}, bf16[169,4]{0,1:T(4,128)(2,1)}, u32[]{:S(2)}) copy-start(bf16[169,4]{0,1:T(4,128)(2,1)} %param.23) | copy-start | bytes 4060
Sparse Core Ops, SparseCore 0:
  13.2 67.2 all-gather.4
  172.0 111.5 reduce-scatter.8
  286.8 65.0 all-gather.6
  353.3 63.1 all-gather.8
  429.3 111.5 reduce-scatter.12
  543.1 113.4 reduce-scatter.10
  662.0 65.0 all-gather.10
  730.1 32.7 reduce-scatter.22
  766.0 34.1 reduce-scatter.20
  826.4 32.2 reduce-scatter.18
  862.4 33.8 reduce-scatter.16
  898.5 112.8 reduce-scatter.14
where the time goes:
time: 1070 us; the launch traced here: 1060 us
  waiting for transfers between devices  682 us (64%)
  local copies, waits for them, and re-layouts  127 us (12%)
  blocking collectives  95.4 us (9%)
  matrix products  85.5 us (8%)
  other arithmetic  58.1 us (5%)
  between operations  16 us (1%)
    reduce_scatter x4, waiting for transfers between devices, share_rows(): return lax.psum_scatter(term, 'gy', scatter_dimension=0, tiled=True)  442 us
    all_gather x4, waiting for transfers between devices, full_rows(): return lax.all_gather(part_rows, 'gy', axis=0, tiled=True)  200 us
    psum x1, blocking collectives, blocked_layer(): lax.psum((d_ln1_gain, d_ln1_bias, d_proj_bias, d_ln2_gain, d_ln2_bias, d_...  40.9 us
    reduce_scatter x1, waiting for transfers between devices, blocked_layer(): lax.psum_scatter(d_qkv_weight.astype(jnp.bfloat16), 'gx', scatter_dimensi...  36.2 us
    dot_general x4, matrix products, matmul(): return jnp.dot(left, right, preferred_element_type=jnp.float32)  22.4 us
  transfers between devices with their start and end apart: 12, of which 10 were waited for; matrix products, arithmetic and copies ran while one was open for 14% of the time, Pallas kernels for 0%

commit v1 on v0

v1 whole, which is shorter than its diff:
```python
import jax
import jax.numpy as jnp
from jax import lax
import numpy as np
from jax.experimental import pallas as pl
from jax.experimental.pallas import tpu as pltpu
from jax.sharding import PartitionSpec as P

HD = 32
GRID = 14
WIN = 7
SHIFT = 3
RELS = 169


eps_norm = 1e-05
mask_value = -100.0
inv_root_two = 0.7071067811865476
inv_root_two_pi = 0.3989422804014327


def matmul(left, right):
    return jnp.dot(left, right, preferred_element_type=jnp.float32)


def matmul_tn(left, right):
    return lax.dot_general(
        left, right, (((0,), (0,)), ((), ())), preferred_element_type=jnp.float32
    )


def matmul_nt(left, right):
    return lax.dot_general(
        left, right, (((1,), (1,)), ((), ())), preferred_element_type=jnp.float32
    )


SLOT = 64
PACK = 8
WIN_COUNT = (GRID // WIN) ** 2
IMAGE = GRID * GRID
ALIGN = 16
STEP = IMAGE // ALIGN * ALIGN
SPAN = STEP + ALIGN
far_below = -1e30


def static_tables(image_count):
    rows = np.arange(WIN_COUNT * SLOT)
    win, place = rows // SLOT, rows % SLOT
    row = (win // (GRID // WIN) * WIN + place // WIN + SHIFT) % GRID
    col = (win % (GRID // WIN) * WIN + place % WIN + SHIFT) % GRID
    token = np.where(place < WIN * WIN, row * GRID + col, -1)
    offset = np.arange(image_count) * (IMAGE - STEP)
    column = np.where(token[None] >= 0, token[None] + offset[:, None], -1)
    places = np.arange(SLOT)
    live = places < WIN * WIN
    pr, pc = places // WIN, places % WIN
    rel = (pr[None, :] - pr[:, None] + WIN - 1) * (2 * WIN - 1) + pc[None, :] - pc[:, None] + WIN - 1
    rel = np.where(live[:, None] & live[None, :], rel, -1)
    cells = np.arange(GRID)
    region = np.where(cells < GRID - WIN, 0, np.where(cells < GRID - SHIFT, 1, 2))
    shifted_row = (win // (GRID // WIN) * WIN + np.minimum(place // WIN, WIN - 1)).reshape(WIN_COUNT, SLOT)
    shifted_col = (win % (GRID // WIN) * WIN + place % WIN).reshape(WIN_COUNT, SLOT)
    ids = region[shifted_row] * 3 + region[shifted_col]
    mask = np.where(ids[:, :, None] == ids[:, None, :], 0.0, mask_value)
    mask = np.where(live[None, None, :] & live[None, :, None], mask, 0.0)
    mask = np.where(live[None, :, None], mask, far_below)
    return column.astype(np.int32), rel.astype(np.int32), mask.astype(np.float32)


def attention_tables(rel_table, image_count):
    column, rel, mask = static_tables(image_count)
    column = jnp.asarray(column)
    spots = jnp.arange(SPAN, dtype=jnp.int32)
    perm = (column[:, :, None] == spots).astype(jnp.bfloat16)
    perm_t = (column[:, None, :] == spots[:, None]).astype(jnp.bfloat16)
    heads = rel_table.shape[1]
    onehot = (jnp.arange(RELS, dtype=jnp.int32)[:, None] == jnp.asarray(rel.reshape(1, -1))).astype(
        jnp.bfloat16
    )
    bias = lax.dot_general(
        rel_table, onehot, (((0,), (0,)), ((), ())), preferred_element_type=jnp.float32
    )
    bias = bias.reshape(heads // PACK, PACK, SLOT, SLOT).transpose(0, 2, 1, 3)
    bias = bias[None] + jnp.asarray(mask)[:, None, :, None, :]
    bias = bias.reshape(WIN_COUNT, heads // PACK, SLOT, PACK * SLOT)
    owner = np.arange(PACK * SLOT)[:, None] // SLOT == np.arange(PACK * HD)[None, :] // HD
    owner = jnp.asarray(owner.astype(np.float32)).astype(jnp.bfloat16)
    return perm, perm_t, bias, owner, onehot


def spread(rows, owner):
    return jnp.concatenate([rows] * PACK, axis=0) * owner


def gather_heads(full):
    lanes = lax.broadcasted_iota(jnp.int32, (SLOT, PACK * HD), 1) // HD
    total = full[:SLOT]
    for h in range(1, PACK):
        total = jnp.where(lanes == h, full[h * SLOT : (h + 1) * SLOT], total)
    return total


def forward_kernel(qkv_ref, perm_ref, perm_t_ref, bias_ref, owner_ref, context_ref, windows_ref, probs_ref, ctx_ref):
    image = pl.program_id(0)
    width = context_ref.shape[1]
    groups = width // (PACK * HD)
    start = pl.multiple_of(image * STEP, ALIGN)
    windows_ref[0] = matmul(perm_ref[0], qkv_ref[pl.ds(start, SPAN), :]).astype(jnp.bfloat16)
    for w in range(WIN_COUNT):
        rows = slice(w * SLOT, (w + 1) * SLOT)
        for g in range(groups):
            low = g * PACK * HD
            query = windows_ref[0, rows, low : low + PACK * HD]
            keys = windows_ref[0, rows, width + low : width + low + PACK * HD]
            values = windows_ref[0, rows, 2 * width + low : 2 * width + low + PACK * HD]
            scores = matmul_nt(keys, spread(query, owner_ref[...])) * HD ** (-0.5) + bias_ref[w, g]
            raised = jnp.exp(scores - jnp.max(scores, 0, keepdims=True))
            probs = raised * (1.0 / jnp.sum(raised, 0, keepdims=True))
            probs_ref[0, w * groups + g] = probs
            full = matmul_tn(probs.astype(jnp.bfloat16), values)
            ctx_ref[rows, low : low + PACK * HD] = gather_heads(full).astype(jnp.bfloat16)

    @pl.when(image == 0)
    def _():
        context_ref[...] = jnp.zeros_like(context_ref)

    context_ref[pl.ds(start, SPAN), :] += matmul(perm_t_ref[0], ctx_ref[...]).astype(jnp.bfloat16)


def backward_kernel(
    d_context_ref, windows_ref, probs_ref, perm_ref, perm_t_ref, owner_ref,
    d_mixed_ref, d_bias_ref, d_qv_ref, d_ctx_ref, d_win_ref,
):
    image = pl.program_id(0)
    width = d_context_ref.shape[1]
    groups = width // (PACK * HD)
    start = pl.multiple_of(image * STEP, ALIGN)

    @pl.when(image == 0)
    def _():
        d_mixed_ref[...] = jnp.zeros_like(d_mixed_ref)
        d_bias_ref[...] = jnp.zeros_like(d_bias_ref)
        d_qv_ref[...] = jnp.zeros_like(d_qv_ref)

    d_ctx_ref[...] = matmul(perm_ref[0], d_context_ref[pl.ds(start, SPAN), :]).astype(jnp.bfloat16)
    for g in range(groups):
        low = g * PACK * HD
        cols = slice(low, low + PACK * HD)
        d_bias = jnp.zeros((SLOT, PACK * SLOT), jnp.float32)
        d_query_sum = jnp.zeros((1, PACK * HD), jnp.float32)
        d_value_sum = jnp.zeros((1, PACK * HD), jnp.float32)
        for w in range(WIN_COUNT):
            rows = slice(w * SLOT, (w + 1) * SLOT)
            query = windows_ref[0, rows, low : low + PACK * HD]
            keys = windows_ref[0, rows, width + low : width + low + PACK * HD]
            values = windows_ref[0, rows, 2 * width + low : 2 * width + low + PACK * HD]
            probs = probs_ref[0, w * groups + g]
            d_wide = spread(d_ctx_ref[rows, cols], owner_ref[...])
            d_probs = matmul_nt(values, d_wide)
            d_values = matmul(probs.astype(jnp.bfloat16), d_wide)
            d_scores = probs * (d_probs - jnp.sum(probs * d_probs, 0, keepdims=True))
            d_bias = d_bias + d_scores
            d_low = d_scores.astype(jnp.bfloat16)
            d_keys = matmul(d_low, spread(query, owner_ref[...])) * HD ** (-0.5)
            d_query = gather_heads(matmul_tn(d_low, keys)) * HD ** (-0.5)
            d_win_ref[rows, low : low + PACK * HD] = d_query.astype(jnp.bfloat16)
            d_win_ref[rows, width + low : width + low + PACK * HD] = d_keys.astype(jnp.bfloat16)
            d_win_ref[rows, 2 * width + low : 2 * width + low + PACK * HD] = d_values.astype(jnp.bfloat16)
            d_query_sum = d_query_sum + jnp.sum(d_query, 0, keepdims=True)
            d_value_sum = d_value_sum + jnp.sum(d_values, 0, keepdims=True)
        d_bias_ref[g] += d_bias
        d_qv_ref[0:1, cols] += d_query_sum
        d_qv_ref[1:2, cols] += d_value_sum
    d_mixed_ref[pl.ds(start, SPAN), :] += matmul(perm_t_ref[0], d_win_ref[...]).astype(jnp.bfloat16)


def whole(shape):
    return pl.BlockSpec(shape, lambda n: (0,) * len(shape))


def per_image(shape):
    return pl.BlockSpec((1,) + shape, lambda n: (n,) + (0,) * len(shape))


def attend_forward(qkv, tables):
    perm, perm_t, bias, owner, _ = tables
    tok, wide = qkv.shape
    width = wide // 3
    count, spots = perm.shape[:2]
    tiles = WIN_COUNT * width // (PACK * HD)
    return pl.pallas_call(
        forward_kernel,
        grid=(count,),
        in_specs=[whole(qkv.shape), per_image((spots, SPAN)), per_image((SPAN, spots)), whole(bias.shape), whole(owner.shape)],
        out_specs=[whole((tok, width)), per_image((spots, wide)), per_image((tiles, SLOT, PACK * SLOT))],
        out_shape=[
            jax.ShapeDtypeStruct((tok, width), jnp.bfloat16),
            jax.ShapeDtypeStruct((count, spots, wide), jnp.bfloat16),
            jax.ShapeDtypeStruct((count, tiles, SLOT, PACK * SLOT), jnp.float32),
        ],
        scratch_shapes=[pltpu.VMEM((spots, width), jnp.bfloat16)],
        name="attend_forward",
    )(qkv, perm, perm_t, bias, owner)


def attend_backward(d_context, windows, probs, tables):
    perm, perm_t, _, owner, onehot = tables
    tok, width = d_context.shape
    count, spots, wide = windows.shape
    groups = width // (PACK * HD)
    tiles = probs.shape[1]
    d_mixed, d_bias, d_qv = pl.pallas_call(
        backward_kernel,
        grid=(count,),
        in_specs=[
            whole(d_context.shape), per_image((spots, wide)), per_image((tiles, SLOT, PACK * SLOT)),
            per_image((spots, SPAN)), per_image((SPAN, spots)), whole(owner.shape),
        ],
        out_specs=[whole((tok, wide)), whole((groups, SLOT, PACK * SLOT)), whole((2, width))],
        out_shape=[
            jax.ShapeDtypeStruct((tok, wide), jnp.bfloat16),
            jax.ShapeDtypeStruct((groups, SLOT, PACK * SLOT), jnp.float32),
            jax.ShapeDtypeStruct((2, width), jnp.float32),
        ],
        scratch_shapes=[pltpu.VMEM((spots, width), jnp.bfloat16), pltpu.VMEM((spots, wide), jnp.bfloat16)],
        name="attend_backward",
    )(d_context, windows, probs, perm, perm_t, owner)
    d_bias = d_bias.reshape(groups, SLOT, PACK, SLOT).transpose(0, 2, 1, 3).reshape(groups * PACK, SLOT * SLOT)
    d_table = lax.dot_general(
        onehot.astype(jnp.float32), d_bias, (((1,), (1,)), ((), ())), precision=lax.Precision.HIGHEST
    )
    return d_mixed, d_qv, d_table


def gelu_parts(pre_act):
    cdf_part = 0.5 * (1.0 + jax.scipy.special.erf(pre_act * inv_root_two))
    return (
        pre_act * cdf_part,
        cdf_part + pre_act * jnp.exp(-0.5 * pre_act * pre_act) * inv_root_two_pi,
    )


def layer_norm(rows, gain, shift):
    row_mean = jnp.mean(rows, -1, keepdims=True)
    row_var = jnp.mean(rows * rows, -1, keepdims=True) - row_mean * row_mean
    inv_std = lax.rsqrt(row_var + eps_norm)
    normed = (rows - row_mean) * inv_std
    return (normed, inv_std, normed * gain + shift)


def norm_back(d_out, normed, inv_std, gain):
    d_normed = d_out * gain
    return inv_std * (
        d_normed
        - jnp.mean(d_normed, -1, keepdims=True)
        - normed * jnp.mean(d_normed * normed, -1, keepdims=True)
    )


def whole_matrix(block, gx_dim, gy_dim):
    both = lax.all_gather(block, ("gx", "gy"), axis=0, tiled=False)
    gx_size, gy_size = lax.axis_size("gx"), lax.axis_size("gy")
    both = both.reshape((gx_size, gy_size) + block.shape)
    shape = [d for d in block.shape]
    if gx_dim < gy_dim:
        if block.ndim == 3:
            out = both.transpose(0, 2, 3, 1, 4)
        else:
            out = both.transpose(0, 2, 1, 3)
    else:
        out = both.transpose(1, 2, 0, 3)
    shape[gx_dim] *= gx_size
    shape[gy_dim] *= gy_size
    return out.reshape(shape)


def share_matrix(grad, gx_dim, gy_dim):
    gx_size, gy_size = lax.axis_size("gx"), lax.axis_size("gy")
    grad = grad.astype(jnp.bfloat16)
    if grad.ndim == 3:
        a, b, c = grad.shape
        blocks = grad.reshape(gx_size, a // gx_size, b, gy_size, c // gy_size).transpose(0, 3, 1, 2, 4)
    elif gx_dim < gy_dim:
        a, c = grad.shape
        blocks = grad.reshape(gx_size, a // gx_size, gy_size, c // gy_size).transpose(0, 2, 1, 3)
    else:
        a, c = grad.shape
        blocks = grad.reshape(gy_size, a // gy_size, gx_size, c // gx_size).transpose(2, 0, 1, 3)
    blocks = blocks.reshape((gx_size * gy_size,) + blocks.shape[2:])
    mine = lax.psum_scatter(blocks, ("gx", "gy"), scatter_dimension=0, tiled=False)
    return mine.astype(jnp.float32)


def own_columns(summed, axis):
    size = summed.shape[axis] // lax.axis_size("gy")
    return lax.dynamic_slice_in_dim(summed, lax.axis_index("gy") * size, size, axis)


def local_live(tok_local, live_images):
    position = lax.axis_index("gy")
    per_device = tok_local // (GRID * GRID)
    slot_index = position * per_device + jnp.arange(tok_local, dtype=jnp.int32) // (GRID * GRID)
    return slot_index < live_images[0]


def blocked_layer(block_input, cotangent, live_images, params):
    (
        ln1_gain,
        ln1_bias,
        qkv_weight,
        qv_bias,
        rel_table,
        proj_weight,
        proj_bias,
        ln2_gain,
        ln2_bias,
        fc1_weight,
        fc1_bias,
        fc2_weight,
        fc2_bias,
    ) = params
    tok_local, width = block_input.shape
    qkv_rows = whole_matrix(qkv_weight, 0, 2)
    proj_cols = whole_matrix(proj_weight, 1, 0)
    fc1_rows = whole_matrix(fc1_weight, 0, 1)
    fc2_cols = whole_matrix(fc2_weight, 1, 0)
    qv_bias = lax.all_gather(qv_bias, "gy", axis=1, tiled=True)
    rel_table = lax.all_gather(rel_table, "gy", axis=1, tiled=True)
    fc1_bias = lax.all_gather(fc1_bias, "gy", axis=0, tiled=True)
    feat_local = width
    qkv_flat = qkv_rows.reshape(width, 3 * feat_local)
    gain_one = ln1_gain.astype(jnp.float32)
    gain_two = ln2_gain.astype(jnp.float32)
    resid = block_input.astype(jnp.float32)
    normed_one, scale_one, pre_one = layer_norm(resid, gain_one, ln1_bias.astype(jnp.float32))
    hidden_one = (pre_one.astype(jnp.bfloat16))
    bias_row = jnp.stack([qv_bias[0], jnp.zeros_like(qv_bias[0]), qv_bias[1]]).reshape(1, 3 * width)
    mixed = (matmul(hidden_one, qkv_flat) + bias_row.astype(jnp.float32)).astype(jnp.bfloat16)
    tables = attention_tables(rel_table, tok_local // IMAGE)
    context, windows, probs = attend_forward(mixed, tables)
    resid_one = resid + (matmul(context, proj_cols)) + proj_bias.astype(jnp.float32)
    normed_two, scale_two, pre_two = layer_norm(resid_one, gain_two, ln2_bias.astype(jnp.float32))
    hidden_two = (pre_two.astype(jnp.bfloat16))
    pre_act = matmul(hidden_two, fc1_rows) + fc1_bias.astype(jnp.float32)
    act_full, slope = gelu_parts(pre_act)
    act_low = act_full.astype(jnp.bfloat16)
    output = (
        resid_one + (matmul(act_low, fc2_cols)) + fc2_bias.astype(jnp.float32)
    ).astype(jnp.bfloat16)
    live_rows = local_live(tok_local, live_images)
    grad_out = jnp.where(live_rows[:, None], cotangent, jnp.zeros_like(cotangent))
    grad_float = grad_out.astype(jnp.float32)
    grad_full = (grad_out)
    d_fc2_bias = jnp.sum(grad_float, 0)
    d_fc2_weight = matmul_tn(act_low, grad_full)
    d_pre = matmul_nt(grad_full, fc2_cols) * slope
    d_fc1_bias = jnp.sum(d_pre, 0)
    d_pre_low = d_pre.astype(jnp.bfloat16)
    d_fc1_weight = matmul_tn(hidden_two, d_pre_low)
    d_hidden_two = (matmul_nt(d_pre_low, fc1_rows))
    d_ln2_gain = jnp.sum(d_hidden_two * normed_two, 0)
    d_ln2_bias = jnp.sum(d_hidden_two, 0)
    d_resid_one = grad_float + norm_back(d_hidden_two, normed_two, scale_two, gain_two)
    d_proj_bias = jnp.sum(d_resid_one, 0)
    d_resid_full = (d_resid_one.astype(jnp.bfloat16))
    d_proj_weight = matmul_tn(context, d_resid_full)
    d_context = matmul_nt(d_resid_full, proj_cols).astype(jnp.bfloat16)
    d_mixed, d_qv_bias, d_table = attend_backward(d_context, windows, probs, tables)
    d_qkv_weight = matmul_tn(hidden_one, d_mixed).reshape(width, 3, feat_local)
    d_hidden_one = (matmul_nt(d_mixed, qkv_flat))
    d_ln1_gain = jnp.sum(d_hidden_one * normed_one, 0)
    d_ln1_bias = jnp.sum(d_hidden_one, 0)
    d_input = (d_resid_one + norm_back(d_hidden_one, normed_one, scale_one, gain_one)).astype(
        jnp.bfloat16
    )
    d_fc2_weight = share_matrix(d_fc2_weight, 1, 0)
    d_fc1_weight = share_matrix(d_fc1_weight, 0, 1)
    d_proj_weight = share_matrix(d_proj_weight, 1, 0)
    d_qkv_weight = share_matrix(d_qkv_weight, 0, 2)
    sums = lax.psum(
        (d_ln1_gain, d_ln1_bias, d_proj_bias, d_ln2_gain, d_ln2_bias, d_fc2_bias,
         d_qv_bias, d_table, d_fc1_bias), ("gx", "gy")
    )
    norm_sums = sums[:6]
    head_sums = (own_columns(sums[6], 1), own_columns(sums[7], 1), own_columns(sums[8], 0))
    return (
        output,
        d_input,
        norm_sums[0],
        norm_sums[1],
        d_qkv_weight,
        head_sums[0],
        head_sums[1],
        d_proj_weight,
        norm_sums[2],
        norm_sums[3],
        norm_sums[4],
        d_fc1_weight,
        head_sums[2],
        d_fc2_weight,
        norm_sums[5],
    )


def shards(
    block_input,
    cotangent,
    live_images,
    ln1_gain,
    ln1_bias,
    qkv_weight,
    qv_bias,
    rel_table,
    proj_weight,
    proj_bias,
    ln2_gain,
    ln2_bias,
    fc1_weight,
    fc1_bias,
    fc2_weight,
    fc2_bias,
):
    params = (
        ln1_gain,
        ln1_bias,
        qkv_weight,
        qv_bias,
        rel_table,
        proj_weight,
        proj_bias,
        ln2_gain,
        ln2_bias,
        fc1_weight,
        fc1_bias,
        fc2_weight,
        fc2_bias,
    )
    results = blocked_layer(block_input, cotangent, live_images, params)
    return results


def solution(mesh):
    return jax.shard_map(
        shards,
        mesh=mesh,
        in_specs=(
            P(("gx", "gy"), None),
            P(("gx", "gy"), None),
            P("gx"),
            P(),
            P(),
            P("gx", None, "gy"),
            P(None, "gy"),
            P(None, "gy"),
            P("gy", "gx"),
            P(),
            P(),
            P(),
            P("gx", "gy"),
            P("gy"),
            P("gy", "gx"),
            P(),
        ),
        out_specs=(
            P(("gx", "gy"), None),
            P(("gx", "gy"), None),
            P(),
            P(),
            P("gx", None, "gy"),
            P(None, "gy"),
            P(None, "gy"),
            P("gy", "gx"),
            P(),
            P(),
            P(),
            P("gx", "gy"),
            P("gy"),
            P("gy", "gx"),
            P(),
        ),
        check_vma=False,
    )
```

time: 1070 us -> 744 us (0.70)
  waiting for transfers between devices: 682 us -> 420 us
  local copies, waits for them, and re-layouts: 127 us -> 60.7 us
  blocking collectives: 95.4 us -> 147 us
  other arithmetic: 58.1 us -> 14.8 us
  matrix products: 85.5 us -> 51.5 us
  Pallas kernels: 0 us -> 27.3 us
    all_gather x4 -> x3, waiting for transfers between devices: 200 us -> 31.8 us  [whole_matrix(): both = lax.all_gather(block, ('gx', 'gy'), axis=0, tiled=False)]
    reduce_scatter x8 -> x4, waiting for transfers between devices: 481 us -> 386 us  [share_matrix(): lax.psum_scatter(blocks, ('gx', 'gy'), scatter_dimension=0, tiled=False)]
    all_gather x4, blocking collectives: 40 us -> 106 us  [the longest x1 69.3 us: whole_matrix(): both = lax.all_gather(block, ('gx', 'gy'), axis=0, tiled=False)]
    pallas_call x0 -> x2, Pallas kernels: none -> 27.3 us  [the longest x1 15.7 us: attend_backward(): pl.pallas_call(backward_kernel, grid=(count,), in_specs=[whole(d_context....]
    dot_general x8 -> x2, matrix products: 24.3 us -> 2.72 us  [the longest x1 1.41 us: attend_backward(): lax.dot_general(onehot.astype(jnp.float32), d_bias, (((1,), (1,)), ((), (...]
    slice x23 -> x1, local copies, waits for them, and re-layouts: 18.4 us -> 0.01 us  [blocked_layer(): qv_bias[0]]
    reduce_sum x9 -> x0, other arithmetic: 15.5 us -> none  [the longest x4 4.48 us: blocked_layer(): d_qv_bias = jnp.stack([jnp.sum(d_query, 0), jnp.sum(d_values, 0)])]
    psum x1 -> x0, blocking collectives: 14.4 us -> none  [blocked_layer(): head_sums = lax.psum((d_qv_bias, d_table, d_fc1_bias), 'gx')]
  transfers between devices with their start and end apart: 12 -> 7, of which waited for: 10 -> 5; matrix products, arithmetic and copies ran while one was open for 14% -> 13% of each run, Pallas kernels for 0% -> 4%
where the time goes in v1:
time: 744 us; the launch traced here: 738 us
  waiting for transfers between devices  420 us (56%)
  blocking collectives  147 us (20%)
  local copies, waits for them, and re-layouts  60.7 us (8%)
  matrix products  51.5 us (7%)
  Pallas kernels  27.3 us (4%)
  between operations  15.6 us (2%)
  other arithmetic  14.8 us (2%)
    reduce_scatter x4, waiting for transfers between devices, share_matrix(): lax.psum_scatter(blocks, ('gx', 'gy'), scatter_dimension=0, tiled=False)  386 us
    all_gather x1, blocking collectives, whole_matrix(): both = lax.all_gather(block, ('gx', 'gy'), axis=0, tiled=False)  69.3 us
    psum x1, blocking collectives, blocked_layer(): lax.psum((d_ln1_gain, d_ln1_bias, d_proj_bias, d_ln2_gain, d_ln2_bias, d_...  41.2 us
    all_gather x3, waiting for transfers between devices, whole_matrix(): both = lax.all_gather(block, ('gx', 'gy'), axis=0, tiled=False)  31.8 us
    dot_general x4, matrix products, matmul_tn(): lax.dot_general(left, right, (((0,), (0,)), ((), ())), preferred_element_...  18.4 us
    pallas_call x1, Pallas kernels, attend_backward(): pl.pallas_call(backward_kernel, grid=(count,), in_specs=[whole(d_context....  15.7 us
    dot_general x4, matrix products, matmul_nt(): lax.dot_general(left, right, (((1,), (1,)), ((), ())), preferred_element_...  15.4 us
    dot_general x4, matrix products, matmul(): return jnp.dot(left, right, preferred_element_type=jnp.float32)  15 us
  transfers between devices with their start and end apart: 7, of which 5 were waited for; matrix products, arithmetic and copies ran while one was open for 13% of the time, Pallas kernels for 4%

profile of v1, /device:TPU:0, one launch (start us, length us, event | category | flops | bytes accessed | tf_op | source)
XLA Modules:
  0.0 737.7 jit_solution(4468605256912170523)
XLA Ops:
  7.2 0.7 all-gather.10.cloned.1.call-update
  8.0 0.7 all-gather.12.cloned.1.call-update
  8.7 0.7 all-gather.14.cloned.1.call-update
  9.4 0.7 convert_element_type.117
  10.2 12.8 %all_gather.35 = bf16[2,512]{1,0:T(2,128)(2,1)S(1)} all-gather(bf16[2,128]{1,0:T(2,128)(2,1)} %param.26), channel_id=1, replica_groups=mesh['gx'=8,'gy'=4] {'gy'}, dimensions={1}, use_global_device_ids=true | all-gather | bytes 2560 | tf_op jit(solution)/shard_map/all_gather | solution.py:329
  23.1 0.7 convert_element_type.118
  23.8 12.1 %all-gather.4 = bf16[4,4,169]{2,1,0:T(4,128)(2,1)S(1)} all-gather(bf16[1,4,169]{2,1,0:T(4,128)(2,1)} %bitcast.113), channel_id=1, replica_groups=mesh['gx'=8,'gy'=4] {'gy'}, dimensions={0}, use_global_device_ids=true | all-gather | bytes 6760 | tf_op jit(solution)/shard_map/all_gather | solution.py:330
  35.9 1.3 convolution_bitcast_fusion
  38.5 69.3 %all-gather.1 = bf16[4096,64]{0,1:T(8,128)(2,1)S(1)} all-gather(bf16[128,64]{0,1:T(8,128)(2,1)S(1)} %copy-done.11), channel_id=3, replica_groups=mesh['gx'=8,'gy'=4] {'gx','gy'}, dimensions={0}, use_global_device_ids=true | all-gather | bytes 540672 | tf_op jit(solution)/shard_map/all_gather | solution.py:263
  108.1 1.0 copy.64
  109.2 11.9 %all-gather.5 = bf16[4,1,512]{2,1,0:T(2,128)(2,1)S(1)} all-gather(bf16[1,1,512]{2,1,0:T(2,128)(2,1)S(1)} %reshape.217), channel_id=1, replica_groups=mesh['gx'=8,'gy'=4] {'gy'}, dimensions={0}, use_global_device_ids=true | all-gather | bytes 5120 | tf_op jit(solution)/shard_map/all_gather | solution.py:331
  122.2 0.9 fusion.27.perm_t_ref
  123.0 1.0 fusion.26.perm_ref
  124.0 1.1 broadcast_add_fusion.bias_ref
  125.2 2.7 copy.89
  127.8 1.7 reshape_reshape.3
  129.5 4.4 add_convert_fusion.qkv_ref
  133.9 11.6 %attend_forward.1 = (bf16[784,512]{1,0:T(8,128)(2,1)}, bf16[4,256,1536]{2,1,0:T(8,128)(2,1)}, f32[4,8,64,512]{3,2,1,0:T(8,128)}) custom-call(bf16[784,1536]{1,0:T(8,128)(2,1)} %add_convert_fusion.qkv_ref, bf16[4,256,208]{2,1,0:T(8,128)(2,1)} %fusion.26.perm_ref, bf16[4,208,256]{2,1,0:T(8,128)(2,1)} %fusion.27.perm_t_ref, ...), custom_call_target="tpu_custom_call" | custom-call | tf_op jit(solution)/shard_map/attend_forward/pallas_call | solution.py:193
  145.5 2.0 fusion.42
  147.5 3.2 copy.65
  150.7 2.0 copy.75
  152.7 31.7 %all-gather.14.cloned.1.call-done = bf16[16384,64]{0,1:T(8,128)(2,1)} async-done(((bf16[512,64]{0,1:T(8,128)(2,1)}), bf16[16384,64]{0,1:T(8,128)(2,1)}) %all-gather.14.cloned.1.call-update) | async-done | bytes 2097168 | tf_op jit(solution)/shard_map/all_gather | solution.py:263
  184.4 4.5 reshape.191
  188.9 2.3 copy.66
  191.2 0.6 copy.76
  191.9 0.9 copy-done.5
  192.8 4.0 multiply_convert_fusion
  196.8 5.4 fusion.45
  202.2 2.3 multiply_reduce_fusion
  204.5 0.9 fusion.43
  205.7 1.5 convolution_convert_fusion.4
  207.2 2.0 copy.69
  209.2 2.0 reshape.196
  211.2 2.0 copy.70
  213.2 2.5 convolution_convert_fusion.3.d_context_ref
  215.8 15.7 %attend_backward.1 = (bf16[784,1536]{1,0:T(8,128)(2,1)}, f32[2,64,512]{2,1,0:T(8,128)}, f32[2,512]{1,0:T(2,128)}) custom-call(bf16[784,512]{1,0:T(8,128)(2,1)} %convolution_convert_fusion.3.d_context_ref, bf16[4,256,1536]{2,1,0:T(8,128)(2,1)} %get-tuple-element.22.windows_ref, f32[4,8,64,512]{3,2,1,0:T(8,128)} %get-tuple-element.23.probs_ref, ...), custom_call_target="tpu_custom_call" | custom-call | tf_op jit(solution)/shard_map/attend_backward/pallas_call | solution.py:214
  231.5 5.1 convolution_convert_fusion.2
  236.6 3.9 convert_element_type.140
  240.5 3.0 copy.67
  243.6 5.8 convolution_convert_fusion.1
  249.4 4.7 reshape.198
  254.1 3.5 copy.71
  257.7 5.9 convolution_convert_fusion
  263.6 4.0 copy.72
  267.6 4.5 reshape.200
  272.1 3.4 copy.73
  275.6 0.6 copy-done.17
  276.5 0.9 reshape.194
  277.4 1.9 copy.90
  279.3 1.2 reshape.195
  280.6 1.4 fusion.5
  282.0 5.2 fusion.18
  287.2 41.2 %all-reduce = (f32[512]{0:T(512)}, f32[512]{0:T(512)}, f32[2,512]{1,0:T(2,128)S(1)}, f32[169,16]{0,1:T(8,128)S(1)}, f32[512]{0:T(512)}, /*index=5*/f32[512]{0:T(...) all-reduce(f32[512]{0:T(512)S(1)} %get-tuple-element.29, ...), channel_id=1, replica_groups=mesh['gx'=8,'gy'=4] {'gx','gy'}, use_global_device_ids=true, to_apply=%region_9.10 | all-reduce | flops 8848 | bytes 70784 | tf_op jit(solution)/shard_map/psum | solution.py:382
  328.4 0.7 dynamic_slice.11
  330.3 3.3 fusion.17
  333.5 4.7 add_convert_fusion.1
  338.2 10.8 %reduce-scatter.7.cloned.1.call-done = bf16[1,128,64]{1,2,0:T(8,128)(2,1)} async-done(((bf16[32,128,64]{1,2,0:T(8,128)(2,1)}), bf16[1,128,64]{1,2,0:T(8,128)(2,1)}) %reduce-scatter.7.cloned.1.call-update) | async-done | bytes 16400 | tf_op jit(solution)/shard_map/reduce_scatter | solution.py:292
  349.0 1.3 bitcast_convert_fusion.3
  350.4 97.7 %reduce-scatter.5.cloned.1.call-done = bf16[1,64,3,128]{3,1,2,0:T(8,128)(2,1)} async-done(((bf16[32,64,3,128]{3,1,2,0:T(8,128)(2,1)}), bf16[1,64,3,128]{3,1,2,0:T(8,128)(2,1)}) %reduce-scatter.5.cloned.1.call-update) | async-done | bytes 49168 | tf_op jit(solution)/shard_map/reduce_scatter | solution.py:292
  448.1 1.4 bitcast_convert_fusion.2
  449.5 139.6 %reduce-scatter.9.cloned.1.call-done = bf16[1,64,512]{2,1,0:T(8,128)(2,1)} async-done(((bf16[32,64,512]{2,1,0:T(8,128)(2,1)}), bf16[1,64,512]{2,1,0:T(8,128)(2,1)}) %reduce-scatter.9.cloned.1.call-update) | async-done | bytes 65552 | tf_op jit(solution)/shard_map/reduce_scatter | solution.py:292
  589.1 1.5 bitcast_convert_fusion.1
  590.6 138.3 %reduce-scatter.11.cloned.1.call-done = bf16[1,512,64]{1,2,0:T(8,128)(2,1)} async-done(((bf16[32,512,64]{1,2,0:T(8,128)(2,1)}), bf16[1,512,64]{1,2,0:T(8,128)(2,1)}) %reduce-scatter.11.cloned.1.call-update) | async-done | bytes 65552 | tf_op jit(solution)/shard_map/reduce_scatter | solution.py:292
  728.9 1.5 bitcast_convert_fusion
  (77 shorter events, 4.2 us)
Async XLA Ops:
  7.2 118.0 %all-gather.10.cloned.1.call-start = ((), (), s32[]{:S(2)}) async-start(), calls=%async_computation.8 | async-start | bytes 1622016 | tf_op jit(solution)/shard_map/all_gather | solution.py:263
  7.9 139.6 %all-gather.12.cloned.1.call-start = ((), (), s32[]{:S(2)}) async-start(), calls=%async_computation.9 | async-start | bytes 2162688 | tf_op jit(solution)/shard_map/all_gather | solution.py:263
  8.7 175.7 %all-gather.14.cloned.1.call-start = ((), (), s32[]{:S(2)}) async-start(), calls=%async_computation.10 | async-start | bytes 2162688 | tf_op jit(solution)/shard_map/all_gather | solution.py:263
  9.4 339.6 %reduce-scatter.7.cloned.1.call-start = ((), (), s32[]{:S(2)}) async-start(), calls=%async_computation.5 | async-start | bytes 540672 | tf_op jit(solution)/shard_map/reduce_scatter | solution.py:292
  35.9 2.0 copy-start.9
  37.7 0.7 copy-start.11
  38.5 70.7 %copy-start.13 = (bf16[512]{0:T(512)(128)(2,1)S(1)}, bf16[512]{0:T(512)(128)(2,1)}, u32[]{:S(2)}) copy-start(bf16[512]{0:T(512)(128)(2,1)} %param.29) | copy-start | bytes 3076
  38.5 70.7 %copy-start.14 = (bf16[512]{0:T(512)(128)(2,1)S(1)}, bf16[512]{0:T(512)(128)(2,1)}, u32[]{:S(2)}) copy-start(bf16[512]{0:T(512)(128)(2,1)} %param.30) | copy-start | bytes 3076
  38.5 70.7 %copy-start.15 = (bf16[512]{0:T(512)(128)(2,1)S(1)}, bf16[512]{0:T(512)(128)(2,1)}, u32[]{:S(2)}) copy-start(bf16[512]{0:T(512)(128)(2,1)} %param.33) | copy-start | bytes 3076
  38.5 82.6 %copy-start.16 = (bf16[512]{0:T(512)(128)(2,1)S(1)}, bf16[512]{0:T(512)(128)(2,1)}, u32[]{:S(2)}) copy-start(bf16[512]{0:T(512)(128)(2,1)} %param.31) | copy-start | bytes 3076
  38.5 83.3 %copy-start.1 = (bf16[784,512]{1,0:T(8,128)(2,1)S(1)}, bf16[784,512]{1,0:T(8,128)(2,1)}, u32[]{:S(2)}) copy-start(bf16[784,512]{1,0:T(8,128)(2,1)} %param.20) | copy-start | bytes 2408452
  107.7 14.4 %copy-start.10 = (s32[4,256]{1,0:T(4,128)S(1)}, s32[4,256]{1,0:T(4,128)}, u32[]{:S(2)}) copy-start(s32[4,256]{1,0:T(4,128)} %constant.61.clone) | copy-start | bytes 12292
  133.9 11.6 %copy-start.2 = (bf16[784,512]{1,0:T(8,128)(2,1)S(1)}, bf16[784,512]{1,0:T(8,128)(2,1)}, u32[]{:S(2)}) copy-start(bf16[784,512]{1,0:T(8,128)(2,1)} %param.20) | copy-start | bytes 2408452
  133.9 11.6 %copy-start.6 = (bf16[8,4,128,64]{2,1,3,0:T(4,128)(2,1)S(1)}, bf16[8,4,128,64]{2,1,3,0:T(4,128)(2,1)}, u32[]{:S(2)}) copy-start(bf16[8,4,128,64]{2,1,3,0:T(4,128)(2,1)} %copy.64) | copy-start | bytes 1572868
  191.2 1.6 copy-start.5
  191.9 5.0 copy-start.3
  192.8 4.0 copy-start.7
  202.2 2.3 copy-start
  204.5 1.1 copy-start.18
  213.2 234.9 %reduce-scatter.5.cloned.1.call-start = ((), (), s32[]{:S(2)}) async-start(), calls=%async_computation.4 | async-start | bytes 1622016 | tf_op jit(solution)/shard_map/reduce_scatter | solution.py:292
  243.5 345.6 %reduce-scatter.9.cloned.1.call-start = ((), (), s32[]{:S(2)}) async-start(), calls=%async_computation.6 | async-start | bytes 2162688 | tf_op jit(solution)/shard_map/reduce_scatter | solution.py:292
  257.6 471.3 %reduce-scatter.11.cloned.1.call-start = ((), (), s32[]{:S(2)}) async-start(), calls=%async_computation.7 | async-start | bytes 2162688 | tf_op jit(solution)/shard_map/reduce_scatter | solution.py:292
  275.5 0.7 copy-start.17
  275.5 1.0 copy-start.8
  275.5 5.0 copy-start.19
  282.0 5.2 copy-start.12
  330.3 3.3 copy-start.4
Sparse Core Ops, SparseCore 0:
  11.0 58.1 all-gather.9
  72.1 55.6 all-gather.11
  130.7 53.6 all-gather.13
  213.3 135.6 reduce-scatter.6
  354.1 93.9 reduce-scatter.4
  450.2 138.8 reduce-scatter.8
  591.4 137.4 reduce-scatter.10
